TPU v7x, 256 devices: a whole 4x4x8 slice. The times are simulated.
256 devices in a mesh: gx: 32 (over z, y_hi, core), gy: 8 (over x, y_lo).
Axes of the slice: x: 4, y: 4 (y_hi: 2, y_lo: 2; y = y_hi * 2 + y_lo), z: 8, core: 2. Of those that a mesh axis runs over, the one named last changes fastest.
Arguments:
- hamiltonian: bfloat16 [64, 16, 8, 128, 128], P('gx', 'gy'), may hold values from -0.078125 to 0.078125
- neighbours: int32 [64, 16, 8], P('gx', 'gy'), may hold values from 0 to 8, as said below
- probe_seeds: int32 [256], replicated, may hold values from 0 to 1073741823
- coefficients: float32 [5], replicated, may hold values from 0.3 to 1
- cotangent: bfloat16 [64, 16, 128, 256], P('gx', 'gy'), may hold values from -6 to 6
Outputs:
- density: float32 [64, 16, 128, 256], P('gx', 'gy')
- grad_hamiltonian: bfloat16 [64, 16, 8, 128, 128], P('gx', 'gy')
Inputs may be any that keep to these rules, and one draw needn't show every extreme that they name: `neighbours`: each block's list holds 8 different codes.
All inputs are finite; a program needn't handle non-finite values.
Results may differ from a plain program's by a relative error of at most 0.0064.
Values may be sent and summed in bfloat16 or wider, within the bound.
A program may use at most 64 MiB of HBM per device.

v0:
```python
import functools

import jax
import jax.numpy as jnp
from jax import lax
from jax.experimental import pallas as pl
from jax.experimental.pallas import tpu as pltpu
from jax.sharding import PartitionSpec as P

MESH = pl.DeviceIdType.MESH
BF16 = jnp.bfloat16
F32 = jnp.float32
B = 128
HALVES = 2


def mm(left, right):
    return jnp.dot(left, right, preferred_element_type=F32)


def mm_nt(left, right):
    return lax.dot_general(left, right, (((1,), (1,)), ((), ())), preferred_element_type=F32)


def joined(ref, *where):
    return jnp.concatenate([ref[(h,) + where] for h in range(HALVES)], axis=1)


class Copy:
    def __init__(self, *args):
        self.args = args
        self.arrived = False

    def make(self):
        src, dst, sems, where, who = self.args
        return pltpu.make_async_remote_copy(
            src_ref=src, dst_ref=dst, send_sem=sems[0].at[where], recv_sem=sems[1].at[where],
            device_id=who, device_id_type=MESH,
        )

    def start(self):
        self.make().start()

    def recv(self):
        if not self.arrived:
            self.arrived = True
            self.make().wait_recv()

    def sent(self):
        self.make().wait_send()


def kernel(
    nx, ny,
    h_hbm, nbr_ref, seed_ref, coef_ref, cot_hbm,
    tp, av, gacc, den_ref,
    h_outer, h_inner, cot_ref,
    hf, ht, tf, af, acc, qf,
    s0, s3, rd, rp, sc, rg,
    fsend, frecv, asend, arecv, isem,
):
    gx = lax.axis_index("gx")
    gy = lax.axis_index("gy")
    odd = lax.rem(gx, 2)
    out_x = lax.rem(gx + nx - 1 + 2 * odd, nx)
    par_x = gx + 1 - 2 * odd
    right_y = lax.rem(gy + 1, ny)
    left_y = lax.rem(gy + ny - 1, ny)
    partner = (par_x, gy)
    right = (gx, right_y)
    left = (gx, left_y)
    diag_r = (out_x, right_y)
    diag_l = (out_x, left_y)

    barrier = pltpu.get_barrier_semaphore()
    for who in (partner, right, left, diag_r, diag_l):
        pl.semaphore_signal(barrier, inc=1, device_id=who, device_id_type=MESH)
    def real_row(a):
        return a + odd * (1 - 2 * a)

    in_cot = pltpu.make_async_copy(cot_hbm, cot_ref, isem.at[0])
    in_h = [
        pltpu.make_async_copy(h_hbm.at[real_row(a)], ref, isem.at[1 + a])
        for a, ref in enumerate((h_outer, h_inner))
    ]
    in_cot.start()
    in_h[0].start()
    in_h[1].start()

    width = tp.shape[4]

    def coef(t):
        return coef_ref[t]

    def signs(rows):
        whole = HALVES * width
        lane_rows = lax.broadcasted_iota(jnp.int32, (B, whole), 0) * jnp.int32(-1640531535)
        seeds = jnp.broadcast_to(seed_ref[...], (B, whole))
        for i in rows:
            ri = i + odd * (3 - 2 * i)
            px = lax.rem(gx * 2 + ri - 1 + 2 * nx, 2 * nx)
            for j in range(4):
                py = lax.rem(gy * 2 + j - 1 + 2 * ny, 2 * ny)
                base = ((px * (2 * ny) + py) * B) * jnp.int32(-1640531535)
                hashed = (lane_rows + base) ^ seeds
                hashed = hashed ^ (hashed >> 15)
                hashed = hashed * jnp.int32(739982445)
                hashed = hashed ^ (hashed >> 12)
                sign = jnp.where((hashed & 128) == 0, 1.0, -1.0).astype(BF16)
                for h in range(HALVES):
                    tp[h, 0, i, j * B : (j + 1) * B] = sign[:, h * width : (h + 1) * width]

    def select(a, d):
        zero = jnp.zeros((B, B), BF16)
        ra = real_row(a)
        rdx = d + odd * (2 - 2 * d)
        hf[a, d, 0:B, 3 * B : 4 * B] = zero
        hf[a, d, B : 2 * B, 0:B] = zero
        ht[a, d, 3 * B : 4 * B, 0:B] = zero
        ht[a, d, 0:B, B : 2 * B] = zero
        for b in range(2):
            for dy in range(3):
                code = rdx * 3 + dy
                place = jnp.int32(0)
                for k in range(8):
                    place = jnp.where(nbr_ref[ra, b, k] == code, k + 1, place)
                found = jnp.where(place > 0, 1.0, 0.0)
                block = (h_outer, h_inner)[a][b, jnp.maximum(place - 1, 0)].astype(F32) * found
                j = b + dy
                hf[a, d, b * B : (b + 1) * B, j * B : (j + 1) * B] = block.astype(BF16)
                ht[a, d, j * B : (j + 1) * B, b * B : (b + 1) * B] = block.T.astype(BF16)

    def blk(ref, c, n=1):
        return ref.at[c * B : (c + n) * B]

    fs = (fsend, frecv)
    fc = {}
    for h in range(HALVES):
        for t in (1, 2, 3):
            t0, t1, t2, t3 = (tp.at[h, t, i] for i in range(4))
            plan = dict(
                r1=(blk(t1, 2), blk(t1, 0), right),
                l1=(blk(t1, 1), blk(t1, 3), left),
                r2=(blk(t2, 2), blk(t2, 0), right),
                l2=(blk(t2, 1), blk(t2, 3), left),
                dra=(blk(t1, 2), blk(t0, 0), diag_r),
                dla=(blk(t1, 1), blk(t0, 3), diag_l),
                drb=(blk(t1, 3), blk(t0, 1), diag_r),
                dlb=(blk(t1, 0), blk(t0, 2), diag_l),
                pa=(blk(t2, 1, 2), blk(t3, 1, 2), partner),
                p0=(blk(t2, 0), blk(t3, 0), partner),
                p3=(blk(t2, 3), blk(t3, 3), partner),
            )
            fc[t, h] = {
                name: Copy(src, dst, fs, (h, t - 1, n), who) for n, (name, (src, dst, who)) in enumerate(plan.items())
            }
    as_ = (asend, arecv)
    ac = {}
    for h in range(HALVES):
        for r in range(3):
            plan = dict(
                dl=(blk(s0.at[h, r], 0, 2), blk(rd.at[h, r], 2, 2), diag_l),
                dr=(blk(s0.at[h, r], 2, 2), blk(rd.at[h, r], 0, 2), diag_r),
                p=(s3.at[h, r], rp.at[h, r], partner),
                l1=(sc.at[h, r, 0, 0], rg.at[h, r, 0, 1], left),
                r1=(sc.at[h, r, 0, 1], rg.at[h, r, 0, 0], right),
                l2=(sc.at[h, r, 1, 0], rg.at[h, r, 1, 1], left),
                r2=(sc.at[h, r, 1, 1], rg.at[h, r, 1, 0], right),
            )
            ac[r, h] = {
                name: Copy(src, dst, as_, (h, r, n), who) for n, (name, (src, dst, who)) in enumerate(plan.items())
            }

    def cot_part(a, b, h):
        return cot_ref[real_row(a), b, :, h * width : (h + 1) * width].astype(F32)

    def adj_first(h):
        for a in range(2):
            for b in range(2):
                av[h, 4, a, b * B : (b + 1) * B] = (coef(4) * cot_part(a, b, h)).astype(BF16)

    def adj_partner(r, h):
        s3[h, r] = mm(ht[1, 2], av[h, 4 - r, 1]).astype(BF16)
        ac[r, h]["p"].start()

    def adj_diagonal(r, h):
        s0[h, r] = mm(ht[0, 0], av[h, 4 - r, 0]).astype(BF16)
        ac[r, h]["dl"].start()
        ac[r, h]["dr"].start()

    def adj_outer(r, h):
        adj_partner(r, h)
        adj_diagonal(r, h)

    def adj_inner(r, h):
        t = 4 - r
        qf[h, 1] = mm(ht[0, 2], av[h, t, 0]) + mm(ht[1, 1], av[h, t, 1])
        qf[h, 0] = mm(ht[0, 1], av[h, t, 0]) + mm(ht[1, 0], av[h, t, 1])

    def adj_side(r, h, a):
        c = ac[r, h]
        got, l, rt = (rd, "l1", "r1") if a == 0 else (rp, "l2", "r2")
        if a == 0:
            c["dl"].recv()
            c["dr"].recv()
        else:
            c["p"].recv()
        sc[h, r, a, 0] = (qf[h, a, 0:B] + got[h, r, 0:B].astype(F32)).astype(BF16)
        c[l].start()
        sc[h, r, a, 1] = (qf[h, a, 3 * B : 4 * B] + got[h, r, 3 * B : 4 * B].astype(F32)).astype(BF16)
        c[rt].start()

    def adj_finish(r, h, a):
        t = 3 - r
        c = ac[r, h]
        got, l, rt = (rd, "l1", "r1") if a == 0 else (rp, "l2", "r2")
        c[l].recv()
        c[rt].recv()
        for b in range(2):
            rows = slice((1 + b) * B, (2 + b) * B)
            own = slice(b * B, (b + 1) * B)
            total = qf[h, a, rows] + got[h, r, rows].astype(F32) + rg[h, r, a, b].astype(F32)
            scale = coef(t) - coef(4) if t == 2 else coef(t)
            value = scale * cot_part(a, b, h) + 2.0 * total
            if t == 1:
                value = value - af[h, a, own]
            if t == 3:
                af[h, a, own] = value
            av[h, t, a, own] = value.astype(BF16)

    def term_row(t, h, a):
        p = t - 1
        value = mm(hf[a, 0], tp[h, p, a]) + mm(hf[a, 1], tp[h, p, a + 1]) + mm(hf[a, 2], tp[h, p, a + 2])
        first = tp[h, 0, a + 1, B : 3 * B].astype(F32)
        if t == 1:
            acc[h, a] = coef(0) * first + coef(1) * value
        else:
            before = first if t == 2 else tf[h, t - 3, a]
            value = 2.0 * value - before
            total = acc[h, a] + coef(t) * value
            if t < 4:
                acc[h, a] = total
            else:
                for b in range(2):
                    den_ref[real_row(a), b, :, h * width : (h + 1) * width] = total[b * B : (b + 1) * B]
        if t < 3:
            tf[h, t - 1, a] = value
        if t < 4:
            tp[h, t, a + 1, B : 3 * B] = value.astype(BF16)
            c = fc[t, h]
            for name in ("r1", "l1", "dra", "dla") if a == 0 else ("pa", "r2", "l2"):
                c[name].start()

    def need(t, h, a):
        if t == 0:
            return
        c = fc[t, h]
        for name in ("r1", "l1", "r2", "l2") + (("dra", "dla", "drb", "dlb") if a == 0 else ("pa", "p0", "p3")):
            c[name].recv()

    def term(t, h):
        order = (0, 1) if t == 1 else (1, 0)
        for a in order:
            need(t - 1, h, a)
            term_row(t, h, a)

    def relay(t, h):
        c = fc[t, h]
        c["r2"].recv()
        c["p0"].start()
        c["l2"].recv()
        c["p3"].start()
        c["r1"].recv()
        c["dlb"].start()
        c["l1"].recv()
        c["drb"].start()

    def side(r, h):
        adj_side(r, h, 1)
        adj_side(r, h, 0)

    def finish(r, h):
        adj_finish(r, h, 1)
        adj_finish(r, h, 0)

    def gradient(t, first=False):
        for a in range(2):
            for d in range(3):
                full = mm_nt(joined(av, t, a), joined(tp, t - 1, a + d))
                for b in range(2):
                    for dy in range(3):
                        j = b + dy
                        piece = full[b * B : (b + 1) * B, j * B : (j + 1) * B]
                        if not first:
                            piece = piece + gacc[a, b, d * 3 + dy]
                        gacc[a, b, d * 3 + dy] = piece

    halves = range(HALVES)
    signs((0, 1, 2))
    in_cot.wait()
    for h in halves:
        adj_first(h)
    in_h[0].wait()
    select(0, 0)
    pl.semaphore_wait(barrier, 5)
    for h in halves:
        adj_diagonal(0, h)
    select(0, 1)
    select(0, 2)
    for h in halves:
        term_row(1, h, 0)
    signs((3,))
    in_h[1].wait()
    select(1, 2)
    for h in halves:
        adj_partner(0, h)
    select(1, 0)
    select(1, 1)
    for h in halves:
        term_row(1, h, 1)
    for h in halves:
        adj_inner(0, h)
    for t in (1, 2, 3):
        r = t - 1
        for h in halves:
            side(r, h)
            relay(t, h)
        if t < 3:
            for h in halves:
                finish(r, h)
                adj_outer(r + 1, h)
                term(t + 1, h)
                adj_inner(r + 1, h)
    gradient(2, first=True)
    gradient(3)
    for h in halves:
        term(4, h)
    gradient(4)
    for h in halves:
        finish(2, h)
    for group in list(fc.values()) + list(ac.values()):
        for one in group.values():
            one.sent()


def last_kernel(tp, av, gacc, den_ref, nbr_hbm, den_hbm, grad_hbm, grad_ref, sums, nbr_ref, osem):
    odd = lax.rem(lax.axis_index("gx"), 2)
    in_nbr = pltpu.make_async_copy(nbr_hbm, nbr_ref, osem.at[5])
    in_nbr.start()
    out_den = pltpu.make_async_copy(den_ref, den_hbm, osem.at[0])
    out_den.start()
    width = tp.shape[4]
    outs = []
    for a in range(2):
        ra = a + odd * (1 - 2 * a)
        for d in range(3):
            full = mm_nt(joined(av, 1, a), joined(tp, 0, a + d))
            for b in range(2):
                for dy in range(3):
                    j = b + dy
                    piece = full[b * B : (b + 1) * B, j * B : (j + 1) * B]
                    total = (piece + 2.0 * gacc[a, b, d * 3 + dy]) * (1.0 / (HALVES * width))
                    sums[a, b, d * 3 + dy] = total.astype(BF16)
        if a == 0:
            in_nbr.wait()
        for b in range(2):
            for k in range(8):
                code = nbr_ref[ra, b, k]
                rdx = code // 3
                mine = rdx + odd * (2 - 2 * rdx)
                grad_ref[a, b, k] = sums[a, b, mine * 3 + code - 3 * rdx]
            one = pltpu.make_async_copy(grad_ref.at[a, b], grad_hbm.at[ra, b], osem.at[1 + 2 * a + b])
            one.start()
            outs.append(one)
    out_den.wait()
    for one in outs:
        one.wait()


def shards(nx, ny, hamiltonian, neighbours, probe_seeds, coefficients, cotangent):
    width = cotangent.shape[3] // HALVES
    whole = pl.BlockSpec(memory_space=pltpu.VMEM)
    scalars = pl.BlockSpec(memory_space=pltpu.SMEM)
    far = pl.BlockSpec(memory_space=pltpu.HBM)
    vmem = pltpu.VMEM
    dma = pltpu.SemaphoreType.DMA
    inside = pl.BlockSpec(memory_space=pltpu.VMEM)
    kept = pl.pallas_call(
        functools.partial(kernel, nx, ny),
        out_shape=(
            vmem((HALVES, 4, 4, 4 * B, width), BF16),
            vmem((HALVES, 5, 2, 2 * B, width), BF16),
            vmem((2, 2, 9, B, B), F32),
            vmem(cotangent.shape, F32),
        ),
        in_specs=[far, scalars, whole, scalars, far],
        out_specs=(inside,) * 4,
        scratch_shapes=[
            vmem(hamiltonian.shape[1:], BF16),
            vmem(hamiltonian.shape[1:], BF16),
            vmem(cotangent.shape, BF16),
            vmem((2, 3, 2 * B, 4 * B), BF16),
            vmem((2, 3, 4 * B, 2 * B), BF16),
            vmem((HALVES, 2, 2, 2 * B, width), F32),
            vmem((HALVES, 2, 2 * B, width), F32),
            vmem((HALVES, 2, 2 * B, width), F32),
            vmem((HALVES, 2, 4 * B, width), F32),
            vmem((HALVES, 3, 4 * B, width), BF16),
            vmem((HALVES, 3, 4 * B, width), BF16),
            vmem((HALVES, 3, 4 * B, width), BF16),
            vmem((HALVES, 3, 4 * B, width), BF16),
            vmem((HALVES, 3, 2, 2, B, width), BF16),
            vmem((HALVES, 3, 2, 2, B, width), BF16),
            dma((HALVES, 3, 11)),
            dma((HALVES, 3, 11)),
            dma((HALVES, 3, 7)),
            dma((HALVES, 3, 7)),
            dma((3,)),
        ],
        compiler_params=pltpu.CompilerParams(
            collective_id=0, has_side_effects=True, vmem_limit_bytes=58654720
        ),
    )(hamiltonian, neighbours, probe_seeds.reshape(1, -1), coefficients, cotangent)
    return pl.pallas_call(
        last_kernel,
        out_shape=(
            jax.ShapeDtypeStruct(cotangent.shape, F32),
            jax.ShapeDtypeStruct(hamiltonian.shape, BF16),
        ),
        in_specs=[inside] * 4 + [far],
        out_specs=(far, far),
        scratch_shapes=[
            vmem(hamiltonian.shape, BF16), vmem((2, 2, 9, B, B), BF16),
            pltpu.SMEM(neighbours.shape, jnp.int32), dma((6,)),
        ],
        compiler_params=pltpu.CompilerParams(vmem_limit_bytes=16 * 1024 * 1024),
    )(*kept, neighbours)


def solution(mesh):
    placed = (
        P("gx", "gy", None, None, None),
        P("gx", "gy", None),
        P(),
        P(),
        P("gx", "gy", None, None),
    )
    return jax.shard_map(
        functools.partial(shards, mesh.shape["gx"], mesh.shape["gy"]),
        mesh=mesh,
        in_specs=placed,
        out_specs=(P("gx", "gy", None, None), P("gx", "gy", None, None, None)),
        check_vma=False,
    )
```

profile of v0, /device:TPU:1, one launch (start us, length us, event | category | flops | bytes accessed | tf_op | source)
XLA Modules:
  0.0 55.5 jit_solution(14756378772968413100)
XLA Ops:
  0.6 52.2 %shard_map.68 = (bf16[2,4,4,512,128]{4,3,2,1,0:T(8,128)(2,1)S(1)}, bf16[2,5,2,256,128]{4,3,2,1,0:T(8,128)(2,1)S(1)}, f32[2,2,9,128,128]{4,3,2,1,0:T(8,128)S(1)}, f32[2,2,128,256]{3,2,1,0:T(8,128)S(1)}) custom-call(bf16[2,2,8,128,128]{4,3,2,1,0:T(8,128)(2,1)} %h_hbm.1, s32[2,2,8]{2,1,0:T(2,128)} %nbr_hbm.1, s32[1,256]{1,0:T(1,128)} %bitcast.1, f32[5]{0:T(128)} %coef_ref.1, ...), custom_call_target="tpu_custom_call" | custom-call | tf_op jit(solution)/shard_map/pallas_call | solution.py:388
  52.9 0.0 copy-start
  52.9 0.7 %copy-done = s32[2,2,8]{2,1,0:T(2,128)S(1)} copy-done((s32[2,2,8]{2,1,0:T(2,128)S(1)}, s32[2,2,8]{2,1,0:T(2,128)}, u32[]{:S(2)}) %copy-start) | copy-done | bytes 152
  53.5 1.9 %shard_map.69 = (f32[2,2,128,256]{3,2,1,0:T(8,128)}, bf16[2,2,8,128,128]{4,3,2,1,0:T(8,128)(2,1)}) custom-call(bf16[2,4,4,512,128]{4,3,2,1,0:T(8,128)(2,1)S(1)} %get-tuple-element.6.tp, bf16[2,5,2,256,128]{4,3,2,1,0:T(8,128)(2,1)S(1)} %get-tuple-element.7.av, f32[2,2,9,128,128]{4,3,2,1,0:T(8,128)S(1)} %get-tuple-element.8.gacc, ...), custom_call_target="tpu_custom_call" | custom-call | tf_op jit(solution)/shard_map/pallas_call | solution.py:424
Async XLA Ops:
  52.9 0.7 %copy-start = (s32[2,2,8]{2,1,0:T(2,128)S(1)}, s32[2,2,8]{2,1,0:T(2,128)}, u32[]{:S(2)}) copy-start(s32[2,2,8]{2,1,0:T(2,128)} %nbr_hbm.1) | copy-start | bytes 388
where the time goes:
time: 56.2 us; the launch traced here: 55.5 us
  Pallas kernels  54.2 us (96%)
  local copies, waits for them, and re-layouts  0.68 us (1%)
  between operations  0.65 us (1%)
    pallas_call x1, Pallas kernels, shards(): pl.pallas_call(functools.partial(kernel, nx, ny), out_shape=(vmem((HALVES...  52.2 us
    pallas_call x1, Pallas kernels, shards(): pl.pallas_call(last_kernel, out_shape=(jax.ShapeDtypeStruct(cotangent.sha...  1.94 us

commit v1 on v0

--- a/solution.py
+++ b/solution.py
@@ -12,6 +12,7 @@
 F32 = jnp.float32
 B = 128
 HALVES = 2
+CUT = 4
 
 
 def mm(left, right):
@@ -52,9 +53,9 @@
 
 def kernel(
     nx, ny,
-    h_hbm, nbr_ref, seed_ref, coef_ref, cot_hbm,
-    tp, av, gacc, den_ref,
-    h_outer, h_inner, cot_ref,
+    h_hbm, nbr_hbm, seed_hbm, coef_hbm, cot_hbm,
+    tp, av, gacc, den_ref, codes,
+    h_outer, h_inner, cot_ref, nbr_ref, seed_ref, coef_ref,
     hf, ht, tf, af, acc, qf,
     s0, s3, rd, rp, sc, rg,
     fsend, frecv, asend, arecv, isem,
@@ -78,14 +79,19 @@
     def real_row(a):
         return a + odd * (1 - 2 * a)
 
-    in_cot = pltpu.make_async_copy(cot_hbm, cot_ref, isem.at[0])
+    in_seed = pltpu.make_async_copy(seed_hbm, seed_ref, isem.at[0])
+    in_nbr = pltpu.make_async_copy(nbr_hbm, nbr_ref, isem.at[1])
+    in_coef = pltpu.make_async_copy(coef_hbm, coef_ref, isem.at[2])
+    in_cot = pltpu.make_async_copy(cot_hbm, cot_ref, isem.at[3])
     in_h = [
-        pltpu.make_async_copy(h_hbm.at[real_row(a)], ref, isem.at[1 + a])
+        [
+            pltpu.make_async_copy(h_hbm.at[real_row(a), b, k : k + CUT], ref.at[b, k : k + CUT], isem.at[4 + a])
+            for b in range(2) for k in range(0, 8, CUT)
+        ]
         for a, ref in enumerate((h_outer, h_inner))
     ]
-    in_cot.start()
-    in_h[0].start()
-    in_h[1].start()
+    for one in [in_seed, in_nbr, in_coef] + in_h[0] + [in_cot] + in_h[1]:
+        one.start()
 
     width = tp.shape[4]
 
@@ -283,9 +289,11 @@
         adj_finish(r, h, 1)
         adj_finish(r, h, 0)
 
-    def gradient(t, first=False):
+    def gradient(t, first=False, outermost=(False, True)):
         for a in range(2):
             for d in range(3):
+                if (a + d == 0) not in outermost:
+                    continue
                 full = mm_nt(joined(av, t, a), joined(tp, t - 1, a + d))
                 for b in range(2):
                     for dy in range(3):
@@ -296,21 +304,27 @@
                         gacc[a, b, d * 3 + dy] = piece
 
     halves = range(HALVES)
+    in_seed.wait()
     signs((0, 1, 2))
+    in_nbr.wait()
+    in_coef.wait()
+    for n in range(32):
+        codes[n : n + 1] = jnp.full((1, B), nbr_ref[n // 16, n // 8 % 2, n % 8], jnp.int32)
     in_cot.wait()
     for h in halves:
         adj_first(h)
-    in_h[0].wait()
+    for one in in_h[0]:
+        one.wait()
     select(0, 0)
-    pl.semaphore_wait(barrier, 5)
-    for h in halves:
-        adj_diagonal(0, h)
     select(0, 1)
     select(0, 2)
-    for h in halves:
+    pl.semaphore_wait(barrier, 5)
+    for h in halves:
+        adj_diagonal(0, h)
         term_row(1, h, 0)
     signs((3,))
-    in_h[1].wait()
+    for one in in_h[1]:
+        one.wait()
     select(1, 2)
     for h in halves:
         adj_partner(0, h)
@@ -330,22 +344,28 @@
                 finish(r, h)
                 adj_outer(r + 1, h)
                 term(t + 1, h)
+            for h in halves:
                 adj_inner(r + 1, h)
     gradient(2, first=True)
     gradient(3)
     for h in halves:
-        term(4, h)
-    gradient(4)
+        need(3, h, 1)
+        term_row(4, h, 1)
+    gradient(4, outermost=(False,))
     for h in halves:
         finish(2, h)
+    for h in halves:
+        need(3, h, 0)
+        term_row(4, h, 0)
+    gradient(4, outermost=(True,))
     for group in list(fc.values()) + list(ac.values()):
         for one in group.values():
             one.sent()
 
 
-def last_kernel(tp, av, gacc, den_ref, nbr_hbm, den_hbm, grad_hbm, grad_ref, sums, nbr_ref, osem):
+def last_kernel(tp, av, gacc, den_ref, codes, den_hbm, grad_hbm, grad_ref, sums, nbr_ref, osem):
     odd = lax.rem(lax.axis_index("gx"), 2)
-    in_nbr = pltpu.make_async_copy(nbr_hbm, nbr_ref, osem.at[5])
+    in_nbr = pltpu.make_async_copy(codes, nbr_ref, osem.at[5])
     in_nbr.start()
     out_den = pltpu.make_async_copy(den_ref, den_hbm, osem.at[0])
     out_den.start()
@@ -365,7 +385,7 @@
             in_nbr.wait()
         for b in range(2):
             for k in range(8):
-                code = nbr_ref[ra, b, k]
+                code = nbr_ref[ra * 16 + b * 8 + k, 0]
                 rdx = code // 3
                 mine = rdx + odd * (2 - 2 * rdx)
                 grad_ref[a, b, k] = sums[a, b, mine * 3 + code - 3 * rdx]
@@ -379,8 +399,6 @@
 
 def shards(nx, ny, hamiltonian, neighbours, probe_seeds, coefficients, cotangent):
     width = cotangent.shape[3] // HALVES
-    whole = pl.BlockSpec(memory_space=pltpu.VMEM)
-    scalars = pl.BlockSpec(memory_space=pltpu.SMEM)
     far = pl.BlockSpec(memory_space=pltpu.HBM)
     vmem = pltpu.VMEM
     dma = pltpu.SemaphoreType.DMA
@@ -392,13 +410,17 @@
             vmem((HALVES, 5, 2, 2 * B, width), BF16),
             vmem((2, 2, 9, B, B), F32),
             vmem(cotangent.shape, F32),
+            vmem((32, B), jnp.int32),
         ),
-        in_specs=[far, scalars, whole, scalars, far],
-        out_specs=(inside,) * 4,
+        in_specs=[far] * 5,
+        out_specs=(inside,) * 5,
         scratch_shapes=[
             vmem(hamiltonian.shape[1:], BF16),
             vmem(hamiltonian.shape[1:], BF16),
             vmem(cotangent.shape, BF16),
+            pltpu.SMEM(neighbours.shape, jnp.int32),
+            vmem((1, probe_seeds.shape[0]), jnp.int32),
+            pltpu.SMEM(coefficients.shape, F32),
             vmem((2, 3, 2 * B, 4 * B), BF16),
             vmem((2, 3, 4 * B, 2 * B), BF16),
             vmem((HALVES, 2, 2, 2 * B, width), F32),
@@ -415,10 +437,10 @@
             dma((HALVES, 3, 11)),
             dma((HALVES, 3, 7)),
             dma((HALVES, 3, 7)),
-            dma((3,)),
+            dma((6,)),
         ],
         compiler_params=pltpu.CompilerParams(
-            collective_id=0, has_side_effects=True, vmem_limit_bytes=58654720
+            collective_id=0, has_side_effects=True, vmem_limit_bytes=58638336
         ),
     )(hamiltonian, neighbours, probe_seeds.reshape(1, -1), coefficients, cotangent)
     return pl.pallas_call(
@@ -427,14 +449,14 @@
             jax.ShapeDtypeStruct(cotangent.shape, F32),
             jax.ShapeDtypeStruct(hamiltonian.shape, BF16),
         ),
-        in_specs=[inside] * 4 + [far],
+        in_specs=[inside] * 5,
         out_specs=(far, far),
         scratch_shapes=[
             vmem(hamiltonian.shape, BF16), vmem((2, 2, 9, B, B), BF16),
-            pltpu.SMEM(neighbours.shape, jnp.int32), dma((6,)),
+            pltpu.SMEM((32, B), jnp.int32), dma((6,)),
         ],
         compiler_params=pltpu.CompilerParams(vmem_limit_bytes=16 * 1024 * 1024),
-    )(*kept, neighbours)
+    )(*kept)
 
 
 def solution(mesh):

time: 56.2 us -> 53.8 us (0.957); the launches traced: 55.5 us -> 53.7 us
  Pallas kernels: 54.2 us -> 53.1 us
  local copies, waits for them, and re-layouts: 0.68 us -> 0 us
    pallas_call x1, Pallas kernels: 52.2 us -> 50.9 us  [shards(): pl.pallas_call(functools.partial(kernel, nx, ny), out_shape=(vmem((HALVES...]
    unnamed x2 -> x0, local copies, waits for them, and re-layouts: 0.68 us -> none
where the time goes in v1:
time: 53.8 us; the launch traced here: 53.7 us
  Pallas kernels  53.1 us (99%)
  between operations  0.64 us (1%)
    pallas_call x1, Pallas kernels, shards(): pl.pallas_call(functools.partial(kernel, nx, ny), out_shape=(vmem((HALVES...  50.9 us
    pallas_call x1, Pallas kernels, shards(): pl.pallas_call(last_kernel, out_shape=(jax.ShapeDtypeStruct(cotangent.sha...  2.18 us

profile of v1, /device:TPU:1, one launch (start us, length us, event | category | flops | bytes accessed | tf_op | source)
XLA Modules:
  0.0 53.7 jit_solution(13754333016050202650)
XLA Ops:
  0.6 50.9 %shard_map.68 = (bf16[2,4,4,512,128]{4,3,2,1,0:T(8,128)(2,1)S(1)}, bf16[2,5,2,256,128]{4,3,2,1,0:T(8,128)(2,1)S(1)}, f32[2,2,9,128,128]{4,3,2,1,0:T(8,128)S(1)},...) custom-call(bf16[2,2,8,128,128]{4,3,2,1,0:T(8,128)(2,1)} %h_hbm.1, s32[2,2,8]{2,1,0:T(2,128)} %nbr_hbm.1, s32[1,256]{1,0:T(1,128)} %bitcast.1, ...), custom_call_target="tpu_custom_call" | custom-call | tf_op jit(solution)/shard_map/pallas_call | solution.py:406
  51.5 2.2 %shard_map.69 = (f32[2,2,128,256]{3,2,1,0:T(8,128)}, bf16[2,2,8,128,128]{4,3,2,1,0:T(8,128)(2,1)}) custom-call(bf16[2,4,4,512,128]{4,3,2,1,0:T(8,128)(2,1)S(1)} %get-tuple-element.7.tp, bf16[2,5,2,256,128]{4,3,2,1,0:T(8,128)(2,1)S(1)} %get-tuple-element.8.av, f32[2,2,9,128,128]{4,3,2,1,0:T(8,128)S(1)} %get-tuple-element.9.gacc, ...), custom_call_target="tpu_custom_call" | custom-call | tf_op jit(solution)/shard_map/pallas_call | solution.py:446

commit v2 on v1

--- a/solution.py
+++ b/solution.py
@@ -341,8 +341,10 @@
             relay(t, h)
         if t < 3:
             for h in halves:
-                finish(r, h)
-                adj_outer(r + 1, h)
+                adj_finish(r, h, 1)
+                adj_partner(r + 1, h)
+                adj_finish(r, h, 0)
+                adj_diagonal(r + 1, h)
                 term(t + 1, h)
             for h in halves:
                 adj_inner(r + 1, h)

time: 53.8 us -> 53.9 us (level); the launches traced: 53.7 us -> 53.2 us
  no operation moved by 1% of the time
where the time goes in v2:
time: 53.9 us; the launch traced here: 53.2 us
  Pallas kernels  52.6 us (98%)
  between operations  0.64 us (1%)
    pallas_call x1, Pallas kernels, shards(): pl.pallas_call(functools.partial(kernel, nx, ny), out_shape=(vmem((HALVES...  50.4 us
    pallas_call x1, Pallas kernels, shards(): pl.pallas_call(last_kernel, out_shape=(jax.ShapeDtypeStruct(cotangent.sha...  2.18 us

profile of v2, /device:TPU:1, one launch (start us, length us, event | category | flops | bytes accessed | tf_op | source)
XLA Modules:
  0.0 53.2 jit_solution(15069323515371753542)
XLA Ops:
  0.6 50.4 %shard_map.68 = (bf16[2,4,4,512,128]{4,3,2,1,0:T(8,128)(2,1)S(1)}, bf16[2,5,2,256,128]{4,3,2,1,0:T(8,128)(2,1)S(1)}, f32[2,2,9,128,128]{4,3,2,1,0:T(8,128)S(1)},...) custom-call(bf16[2,2,8,128,128]{4,3,2,1,0:T(8,128)(2,1)} %h_hbm.1, s32[2,2,8]{2,1,0:T(2,128)} %nbr_hbm.1, s32[1,256]{1,0:T(1,128)} %bitcast.1, ...), custom_call_target="tpu_custom_call" | custom-call | tf_op jit(solution)/shard_map/pallas_call | solution.py:408
  51.0 2.2 %shard_map.69 = (f32[2,2,128,256]{3,2,1,0:T(8,128)}, bf16[2,2,8,128,128]{4,3,2,1,0:T(8,128)(2,1)}) custom-call(bf16[2,4,4,512,128]{4,3,2,1,0:T(8,128)(2,1)S(1)} %get-tuple-element.7.tp, bf16[2,5,2,256,128]{4,3,2,1,0:T(8,128)(2,1)S(1)} %get-tuple-element.8.av, f32[2,2,9,128,128]{4,3,2,1,0:T(8,128)S(1)} %get-tuple-element.9.gacc, ...), custom_call_target="tpu_custom_call" | custom-call | tf_op jit(solution)/shard_map/pallas_call | solution.py:448
